TPU v7x, 32 devices: a whole 2x2x4 slice. The times are simulated.
32 devices in a mesh: groups: 2 (over y), expert: 8 (over z, core), section: 2 (over x), tensor: 1.
Axes of the slice: x: 2, y: 2, z: 4, core: 2. Of those that a mesh axis runs over, the one named last changes fastest.
Arguments:
- opening_residual: bfloat16 [2, 2048, 2048], P('section', ('groups', 'expert'), 'tensor'), parts along dimension 1, may hold values from -12 to 12
- incoming_residual: bfloat16 [1, 2048, 2048], P(None, ('groups', 'expert'), 'tensor'), parts along dimension 1, may hold values from -12 to 12
- stored_summaries: bfloat16 [2, 2, 16, 768, 512], P(None, 'section', ('groups', 'expert')), parts along dimension 2, may hold values from -40 to 40
- stored_counts: int32 [3, 16], P(None, ('groups', 'expert')), parts along dimension 1, may hold values from 1 to 768, as said below
- picked_specialists: int32 [2, 2, 2048, 6], P(None, 'section', ('groups', 'expert')), parts along dimension 2, may hold values from 0 to 15, all different within a row; in each aligned block of 128 rows (0 to 127, 128 to 255, ..., all dimensions but the last counted through in order) at most 64 rows name the same one
- chooser_mixing_share: float32 [2, 2, 2048, 6], P(None, 'section', ('groups', 'expert')), parts along dimension 2, may hold values from 0.05 to 0.4
- mixing_scale_factor: float32 [2, 2048], P('section'), may hold values from 0.25 to 1.75
- asking_projection: bfloat16 [2, 2048, 1024], P('section', None, 'tensor'), may hold values from -0.125 to 0.125
- summary_lookup_factor: bfloat16 [2, 8, 128, 512], P('section', 'tensor'), may hold values from -0.5 to 0.5
- summary_content_factor: bfloat16 [2, 8, 512, 128], P('section', 'tensor'), may hold values from -0.25 to 0.25
- merging_projection: bfloat16 [2, 1024, 2048], P('section', 'tensor'), may hold values from -0.1875 to 0.1875
- compress_projection: bfloat16 [2, 2048, 512], P('section', None, 'tensor'), may hold values from -0.125 to 0.125
- summary_scale_factor: float32 [2, 512], P('section'), may hold values from 0.25 to 1.75
- specialist_scale_factor: float32 [2, 2048], P('section', 'tensor'), may hold values from 0.25 to 1.75
- specialist_switch_factor: bfloat16 [2, 16, 2048, 704], P('section', 'expert', None, 'tensor'), may hold values from -0.125 to 0.125
- specialist_widen_factor: bfloat16 [2, 16, 2048, 704], P('section', 'expert', None, 'tensor'), may hold values from -0.125 to 0.125
- specialist_contract_factor: bfloat16 [2, 16, 704, 2048], P('section', 'expert', 'tensor'), may hold values from -0.21875 to 0.21875
Outputs:
- results: bfloat16 [2, 2, 2048, 2048], P(None, 'section', ('groups', 'expert'), 'tensor'), parts along dimension 2
There are 2 independent parts, one for each index of `groups`. A program takes and returns all parts, laid end to end along the dimension named above; an argument that names none is the same for every part. Nothing has to cross between parts.
Inputs may be any that keep to these rules, and one draw needn't show every extreme that they name: `picked_specialists`: in each aligned block of 128 rows (one sequence) no expert is chosen by more than 64 rows, a bound that some block reaches; each row names 6 different experts. `stored_counts`: in every microbatch some sequence has exactly 768 cached tokens.
All inputs are finite; a program needn't handle non-finite values.
Results may differ from a plain program's by a relative error of at most 0.04.
Values may be sent and summed in bfloat16 or wider, within the bound.
A program may use at most 128 MiB of HBM per device.

v0:
```python
import jax
import jax.numpy as jnp
from jax import lax
from jax.sharding import PartitionSpec as P

CAP = 64
RETURN_CHUNKS = 2
epsilon = 1e-06


def shifted(value, axis, steps):
    count = lax.axis_size(axis)
    initial, last = (max(0, -steps), min(count, count - steps))
    return lax.ppermute(value, axis, [(source, source + steps) for source in range(initial, last)])


def row_norm(values, gain_row):
    return (
        values * lax.rsqrt(jnp.mean(values * values, axis=-1, keepdims=True) + epsilon) * gain_row
    )


def attend(q_lat, cache_rows, new_rows, length, score_scale):
    piece_list = q_lat.shape[0]
    context = cache_rows.shape[0]
    key_rows = jnp.concatenate([cache_rows, new_rows], axis=0)
    scores = (
        jnp.einsum("thl,kl->thk", q_lat, key_rows, preferred_element_type=jnp.float32) * score_scale
    )
    position = lax.broadcasted_iota(jnp.int32, (piece_list, context + piece_list), 1)
    query_pos = lax.broadcasted_iota(jnp.int32, (piece_list, context + piece_list), 0)
    visible = jnp.where(position < context, position < length, position - context <= query_pos)
    scores = jnp.where(visible[:, None, :], scores, -jnp.inf)
    row_max = jnp.max(scores, axis=-1, keepdims=True)
    expd = jnp.where(visible[:, None, :], jnp.exp(scores - row_max), 0.0)
    attention = (expd / jnp.sum(expd, axis=-1, keepdims=True)).astype(jnp.bfloat16)
    return jnp.einsum(
        "thk,kl->thl", attention, key_rows, preferred_element_type=jnp.float32
    ).astype(jnp.bfloat16)


def shards(
    opening_residual,
    incoming_residual,
    stored_summaries,
    stored_counts,
    picked_specialists,
    chooser_mixing_share,
    mixing_scale_factor,
    asking_projection,
    summary_lookup_factor,
    summary_content_factor,
    merging_projection,
    compress_projection,
    summary_scale_factor,
    specialist_scale_factor,
    specialist_switch_factor,
    specialist_widen_factor,
    specialist_contract_factor,
):
    segment_ordinal = lax.axis_index("section")
    section_count = lax.axis_size("section")
    sources = lax.axis_size("expert")
    tick_count = stored_summaries.shape[0]
    piece_list = opening_residual.shape[1]
    inner_feature_midcount = opening_residual.shape[2]
    full_width = mixing_scale_factor.shape[1]
    local_heads = summary_lookup_factor.shape[1]
    head_size = summary_lookup_factor.shape[2]
    top_count = picked_specialists.shape[3]
    expert_local = specialist_switch_factor.shape[1]
    score_scale = head_size ** (-0.5)
    expert_ids = lax.broadcasted_iota(jnp.int32, (1, 1, 1, expert_local * sources), 3)
    shares_dense = jnp.sum(
        jnp.where(
            picked_specialists[:, 0][..., None] == expert_ids,
            chooser_mixing_share[:, 0][..., None],
            0.0,
        ),
        axis=2,
    )
    shares_all = lax.all_gather(jnp.swapaxes(shares_dense, 1, 2), "expert", axis=1, tiled=False)
    mine = lax.dynamic_slice_in_dim(
        shares_all, lax.axis_index("expert") * expert_local, expert_local, axis=2
    )
    chosen = mine > 0.0
    earlier_or_same = (
        lax.broadcasted_iota(jnp.int32, (piece_list, piece_list), 0)
        <= lax.broadcasted_iota(jnp.int32, (piece_list, piece_list), 1)
    ).astype(jnp.bfloat16)
    rank = jnp.einsum(
        "tjer,rq->tjeq",
        chosen.astype(jnp.bfloat16),
        earlier_or_same,
        preferred_element_type=jnp.float32,
    ).astype(jnp.int32)
    slots = lax.broadcasted_iota(jnp.int32, (1, 1, 1, CAP, 1), 3) + 1
    at_slot = (rank[..., None, :] == slots) & chosen[..., None, :]
    placed = at_slot.astype(jnp.bfloat16)
    slot_share = jnp.sum(jnp.where(at_slot, mine[..., None, :], 0.0), axis=-1)
    outputs = []
    present_carry = opening_residual[0]
    section_out = present_carry
    for step_index in range(tick_count):
        if step_index > 0:
            handed = shifted(section_out, "section", 1)
            present_carry = jnp.where(
                segment_ordinal == 0, incoming_residual[step_index - 1], handed
            )
        micro_index = step_index - segment_ordinal + section_count - 1
        length = lax.dynamic_index_in_dim(stored_counts[:, 0], micro_index, 0, keepdims=False)
        full_rows = lax.all_gather(present_carry, "tensor", axis=1, tiled=True)
        normed = row_norm(full_rows.astype(jnp.float32), mixing_scale_factor[0]).astype(
            jnp.bfloat16
        )
        queries = jnp.dot(normed, asking_projection[0], preferred_element_type=jnp.float32).astype(
            jnp.bfloat16
        )
        queries = queries.reshape(piece_list, local_heads, head_size)
        q_lat = jnp.einsum(
            "thd,hdl->thl", queries, summary_lookup_factor[0], preferred_element_type=jnp.float32
        ).astype(jnp.bfloat16)
        latent_part = jnp.dot(normed, compress_projection[0], preferred_element_type=jnp.float32)
        latent_raw = lax.all_gather(
            latent_part.astype(jnp.bfloat16), "tensor", axis=1, tiled=True
        ).astype(latent_part.dtype)
        new_latent = row_norm(latent_raw, summary_scale_factor[0]).astype(jnp.bfloat16)
        o_lat = attend(q_lat, stored_summaries[step_index, 0, 0], new_latent, length, score_scale)
        heads_out = jnp.einsum(
            "thl,hld->thd", o_lat, summary_content_factor[0], preferred_element_type=jnp.float32
        ).astype(jnp.bfloat16)
        heads_out = heads_out.reshape(piece_list, local_heads * head_size)
        head_terms = jnp.dot(heads_out, merging_projection[0], preferred_element_type=jnp.float32)
        residual = present_carry.astype(jnp.float32) + lax.psum_scatter(
            head_terms.astype(jnp.bfloat16), "tensor", scatter_dimension=1, tiled=True
        ).astype(jnp.float32)
        squares = lax.psum(jnp.sum(residual * residual, axis=1), "tensor")
        moe_input = (
            residual
            * lax.rsqrt(squares / full_width + epsilon)[:, None]
            * specialist_scale_factor[0]
        ).astype(jnp.bfloat16)
        whole_rows = lax.all_gather(moe_input, "tensor", axis=1, tiled=True)
        place = placed[step_index]
        share = slot_share[step_index]
        all_rows = lax.all_gather(whole_rows, "expert", axis=0, tiled=True)
        all_rows = all_rows.reshape(sources, piece_list, full_width)
        hidden_list = []
        for e in range(expert_local):
            rows_in = jnp.einsum(
                "jsr,jrd->jsd", place[:, e], all_rows, preferred_element_type=jnp.float32
            ).astype(jnp.bfloat16)
            rows_in = rows_in.reshape(sources * CAP, full_width)
            gate_values = jnp.dot(
                rows_in, specialist_switch_factor[0, e], preferred_element_type=jnp.float32
            )
            up_values = jnp.dot(
                rows_in, specialist_widen_factor[0, e], preferred_element_type=jnp.float32
            )
            hidden_list.append(
                (jax.nn.silu(gate_values) * up_values * share[:, e].reshape(-1, 1)).astype(
                    jnp.bfloat16
                )
            )
        chunk = full_width // RETURN_CHUNKS
        routed_list = []
        for c in range(RETURN_CHUNKS):
            total = None
            for e in range(expert_local):
                down = jnp.dot(
                    hidden_list[e],
                    specialist_contract_factor[0, e][:, c * chunk : (c + 1) * chunk],
                    preferred_element_type=jnp.float32,
                ).astype(jnp.bfloat16)
                term = jnp.einsum(
                    "jsr,jsd->jrd",
                    place[:, e],
                    down.reshape(sources, CAP, chunk),
                    preferred_element_type=jnp.float32,
                )
                total = term if total is None else total + term
            total = total.astype(jnp.bfloat16).reshape(sources * piece_list, chunk)
            routed_list.append(lax.psum_scatter(total, "expert", scatter_dimension=0, tiled=True))
        routed = jnp.concatenate(routed_list, axis=1)
        routed = lax.psum_scatter(routed, "tensor", scatter_dimension=1, tiled=True).astype(
            jnp.float32
        )
        section_out = (residual + routed).astype(jnp.bfloat16)
        outputs.append(section_out)
    return jnp.stack(outputs)[:, None]


def solution(mesh):
    in_specs = (
        P("section", ("groups", "expert"), "tensor"),
        P(None, ("groups", "expert"), "tensor"),
        P(None, "section", ("groups", "expert"), None, None),
        P(None, ("groups", "expert")),
        P(None, "section", ("groups", "expert"), None),
        P(None, "section", ("groups", "expert"), None),
        P("section", None),
        P("section", None, "tensor"),
        P("section", "tensor", None, None),
        P("section", "tensor", None, None),
        P("section", "tensor", None),
        P("section", None, "tensor"),
        P("section", None),
        P("section", "tensor"),
        P("section", "expert", None, "tensor"),
        P("section", "expert", None, "tensor"),
        P("section", "expert", "tensor", None),
    )
    out_specs = P(None, "section", ("groups", "expert"), "tensor")
    return jax.shard_map(shards, mesh=mesh, in_specs=in_specs, out_specs=out_specs, check_vma=False)
```

profile of v0, /device:TPU:0, one launch (start us, length us, event | category | flops | bytes accessed | tf_op | source)
XLA Modules:
  0.0 368.0 jit_solution(13593333180121278280)
XLA Ops:
  11.4 3.0 fusion.130
  20.1 4.5 %fusion.105 = f32[128,8,896]{2,0,1:T(8,128)} fusion(bf16[1,8,128,512]{3,2,1,0:T(8,128)(2,1)S(1)} %copy-done.7, bf16[128,512]{1,0:T(8,128)(2,1)S(1)} %multiply_convert_fusion.3, bf16[768,512]{1,0:T(8,128)(2,1)} %get-tuple-element.10, bf16[16,8,8,128]{3,2,1,0:T(8,128)(2,1)S(1)} %fusion.130), kind=kOutput, calls=%fused_computation.97 | convolution fusion | flops 1076101120 | bytes 5898240 | tf_op jit(solution)/shard_map/thl,kl->thk/dot_general | solution.py:28
  24.6 6.7 %fusion.191 = (f32[128,8]{0,1:T(8,128)S(1)}, f32[128,8,896]{2,0,1:T(8,128)}) fusion(f32[128,8,896]{2,0,1:T(8,128)} %fusion.105, pred[128,896]{1,0:T(8,128)(4,1)} %get-tuple-element.20), kind=kOutput, calls=%fused_computation.204 | output fusion | flops 6423423 | bytes 7458816 | tf_op jit(solution)/shard_map/sub | solution.py:35
  31.3 3.9 %fusion.126 = bf16[8,128,128]{1,2,0:T(8,128)(2,1)S(1)} fusion(f32[128,8,896]{2,0,1:T(8,128)} %get-tuple-element.26, f32[128,8]{0,1:T(8,128)S(1)} %get-tuple-element.25, bf16[1,8,512,128]{3,2,1,0:T(8,128)(2,1)} %param.26, bf16[128,512]{1,0:T(8,128)(2,1)S(1)} %multiply_convert_fusion.3, bf16[768,512]{1,0:T(8,128)(2,1)S(1)} %copy-done.10), kind=kOutput, calls=%fused_computation.116 | convolution fusion | flops 1078067200 | bytes 5902336 | tf_op jit(solution)/shard_map/thl,hld->thd/dot_general | solution.py:129
  35.3 3.1 multiply_reduce_fusion.1
  39.6 16.3 %all-gather = f32[2,128,128]{2,1,0:T(8,128)S(1)} all-gather(f32[2,16,128]{2,1,0:T(8,128)S(1)} %bitcast.305), channel_id=2, replica_groups=mesh['groups'=2,'expert'=8,'section'=2,'tensor'=1] {'expert'}, dimensions={1}, use_global_device_ids=true | all-gather | bytes 147456 | tf_op jit(solution)/shard_map/all_gather | solution.py:82
  57.6 6.3 %slice_bitcast_fusion = (bf16[704,2048]{1,0:T(8,128)(2,1)}, bf16[704,2048]{1,0:T(8,128)(2,1)}) fusion(bf16[1,2,704,2048]{3,2,1,0:T(8,128)(2,1)} %param.33), kind=kLoop, calls=%fused_computation.40 | loop fusion | bytes 11534336 | tf_op jit(solution)/shard_map/squeeze | solution.py:172
  64.0 25.8 %all-gather.4.cloned.1.call-done = bf16[1024,2048]{1,0:T(8,128)(2,1)} async-done(((bf16[128,2048]{1,0:T(8,128)(2,1)}), bf16[1024,2048]{1,0:T(8,128)(2,1)}) %all-gather.4.cloned.1.call-update) | async-done | bytes 4194320 | tf_op jit(solution)/shard_map/all_gather | solution.py:146
  89.8 3.0 convolution_convert_fusion.2
  93.9 3.9 %fusion.16 = f32[512,704]{0,1:T(8,128)S(1)} fusion(bf16[512,2048]{1,0:T(8,128)(2,1)S(1)} %bitcast.286, bf16[1,2,2048,704]{2,3,1,0:T(8,128)(2,1)} %param.31), kind=kOutput, calls=%fused_computation.30 | convolution fusion | flops 1476395008 | bytes 6422528 | tf_op jit(solution)/shard_map/dot_general | solution.py:154
  115.4 27.9 %reduce-scatter.5.cloned.1.call-done = bf16[128,1024]{1,0:T(8,128)(2,1)} async-done(((bf16[1024,1024]{1,0:T(8,128)(2,1)}), bf16[128,1024]{1,0:T(8,128)(2,1)}) %reduce-scatter.5.cloned.1.call-update) | async-done | bytes 262160 | tf_op jit(solution)/shard_map/reduce_scatter | solution.py:183
  143.3 36.7 %reduce-scatter.7.cloned.1.call-done = bf16[128,1024]{1,0:T(8,128)(2,1)} async-done(((bf16[1024,1024]{1,0:T(8,128)(2,1)}), bf16[128,1024]{1,0:T(8,128)(2,1)}) %reduce-scatter.7.cloned.1.call-update) | async-done | bytes 262160 | tf_op jit(solution)/shard_map/reduce_scatter | solution.py:183
  182.0 3.4 collective-permute-start
  185.4 8.5 %collective-permute-done = bf16[128,2048]{1,0:T(8,128)(2,1)S(1)} collective-permute-done((bf16[128,2048]{1,0:T(8,128)(2,1)}, bf16[128,2048]{1,0:T(8,128)(2,1)S(1)}, u32[]{:S(2)}, u32[]{:S(2)}) %collective-permute-start) | collective-permute-done | bytes 524320 | tf_op jit(solution)/shard_map/ppermute | solution.py:14
  195.3 3.2 fusion.127
  199.7 4.5 %fusion.107 = f32[128,8,896]{2,0,1:T(8,128)} fusion(bf16[1,8,128,512]{3,2,1,0:T(8,128)(2,1)S(1)} %copy-done.8, bf16[128,512]{1,0:T(8,128)(2,1)S(1)} %multiply_convert_fusion.2, bf16[768,512]{1,0:T(8,128)(2,1)} %get-tuple-element.9, bf16[16,8,8,128]{3,2,1,0:T(8,128)(2,1)S(1)} %fusion.127), kind=kOutput, calls=%fused_computation.99 | convolution fusion | flops 1076101120 | bytes 5898240 | tf_op jit(solution)/shard_map/thl,kl->thk/dot_general | solution.py:28
  204.2 6.7 %fusion.192 = (f32[128,8]{0,1:T(8,128)S(1)}, f32[128,8,896]{2,0,1:T(8,128)}) fusion(f32[128,8,896]{2,0,1:T(8,128)} %fusion.107, pred[128,896]{1,0:T(8,128)(4,1)S(1)} %copy-done.18), kind=kOutput, calls=%fused_computation.205 | output fusion | flops 6423423 | bytes 7458816 | tf_op jit(solution)/shard_map/sub | solution.py:35
  211.0 3.7 %fusion.125 = bf16[8,128,128]{1,2,0:T(8,128)(2,1)S(1)} fusion(f32[128,8,896]{2,0,1:T(8,128)} %get-tuple-element.32, f32[128,8]{0,1:T(8,128)S(1)} %get-tuple-element.31, bf16[1,8,512,128]{3,2,1,0:T(8,128)(2,1)S(1)} %copy-done.28, bf16[128,512]{1,0:T(8,128)(2,1)S(1)} %multiply_convert_fusion.2, bf16[768,512]{1,0:T(8,128)(2,1)S(1)} %copy-done.9), kind=kOutput, calls=%fused_computation.115 | convolution fusion | flops 1078067200 | bytes 5902336 | tf_op jit(solution)/shard_map/thl,hld->thd/dot_general | solution.py:129
  214.7 3.0 multiply_reduce_fusion
  219.1 48.1 %all-gather.6.cloned.1.call-done = bf16[1024,2048]{1,0:T(8,128)(2,1)} async-done(((bf16[128,2048]{1,0:T(8,128)(2,1)}), bf16[1024,2048]{1,0:T(8,128)(2,1)}) %all-gather.6.cloned.1.call-update) | async-done | bytes 4194320 | tf_op jit(solution)/shard_map/all_gather | solution.py:146
  267.2 3.0 convolution_convert_fusion
  271.4 3.6 fusion.14
  292.6 28.2 %reduce-scatter.9.cloned.1.call-done = bf16[128,1024]{1,0:T(8,128)(2,1)} async-done(((bf16[1024,1024]{1,0:T(8,128)(2,1)}), bf16[128,1024]{1,0:T(8,128)(2,1)}) %reduce-scatter.9.cloned.1.call-update) | async-done | bytes 262160 | tf_op jit(solution)/shard_map/reduce_scatter | solution.py:183
  320.8 36.9 %reduce-scatter.11.cloned.1.call-done = bf16[128,1024]{1,0:T(8,128)(2,1)} async-done(((bf16[1024,1024]{1,0:T(8,128)(2,1)}), bf16[128,1024]{1,0:T(8,128)(2,1)}) %reduce-scatter.11.cloned.1.call-update) | async-done | bytes 262160 | tf_op jit(solution)/shard_map/reduce_scatter | solution.py:183
  (170 shorter events, 59.2 us)
Async XLA Ops:
  6.5 4.8 %copy-start.4 = (bf16[1,128,2048]{2,1,0:T(8,128)(2,1)S(1)}, bf16[1,128,2048]{2,1,0:T(8,128)(2,1)}, u32[]{:S(2)}) copy-start(bf16[1,128,2048]{2,1,0:T(8,128)(2,1)} %param.17) | copy-start | bytes 1572868
  6.5 4.8 %copy-start.19 = (f32[1,2048]{1,0:T(1,128)S(1)}, f32[1,2048]{1,0:T(1,128)}, u32[]{:S(2)}) copy-start(f32[1,2048]{1,0:T(1,128)} %param.23) | copy-start | bytes 24580
  6.5 83.2 %all-gather.4.cloned.1.call-start = ((), (), s32[]{:S(2)}) async-start(), calls=%async_computation.4 | async-start | bytes 4718592 | tf_op jit(solution)/shard_map/all_gather | solution.py:146
  11.3 4.3 %copy-start.27 = (s32[3,1]{0,1:T(1,128)S(1)}, s32[3,1]{0,1:T(1,128)}, u32[]{:S(2)}) copy-start(s32[3,1]{0,1:T(1,128)} %param.20) | copy-start | bytes 40
  11.3 6.1 %copy-start.23 = (f32[1,512]{1,0:T(1,128)S(1)}, f32[1,512]{1,0:T(1,128)}, u32[]{:S(2)}) copy-start(f32[1,512]{1,0:T(1,128)} %param.29) | copy-start | bytes 6148
  14.3 5.7 %copy-start.7 = (bf16[1,8,128,512]{3,2,1,0:T(8,128)(2,1)S(1)}, bf16[1,8,128,512]{3,2,1,0:T(8,128)(2,1)}, u32[]{:S(2)}) copy-start(bf16[1,8,128,512]{3,2,1,0:T(8,128)(2,1)} %param.25) | copy-start | bytes 3145732
  24.6 6.7 %copy-start.10 = (bf16[768,512]{1,0:T(8,128)(2,1)S(1)}, bf16[768,512]{1,0:T(8,128)(2,1)}, u32[]{:S(2)}) copy-start(bf16[768,512]{1,0:T(8,128)(2,1)} %get-tuple-element.10) | copy-start | bytes 2359300
  39.5 103.8 %reduce-scatter.5.cloned.1.call-start = ((), (), s32[]{:S(2)}) async-start(), calls=%async_computation.5 | async-start | bytes 2359296 | tf_op jit(solution)/shard_map/reduce_scatter | solution.py:183
  93.2 4.6 %slice-start = ((s8[5767168]{0:T(1024)(128)(4,1)}), s8[4194304]{0:T(1024)(128)(4,1)S(1)}, s32[]{:S(2)}) async-start(s8[5767168]{0:T(1024)(128)(4,1)} %bitcast.316), calls=%async_computation.10 | async-start | bytes 8388608
  93.9 5.6 %slice-start.4 = ((s8[5767168]{0:T(1024)(128)(4,1)}), s8[4194304]{0:T(1024)(128)(4,1)S(1)}, s32[]{:S(2)}) async-start(s8[5767168]{0:T(1024)(128)(4,1)} %bitcast.320), calls=%async_computation.14 | async-start | bytes 8388608
  108.6 71.4 %reduce-scatter.7.cloned.1.call-start = ((), (), s32[]{:S(2)}) async-start(), calls=%async_computation.6 | async-start | bytes 2359296 | tf_op jit(solution)/shard_map/reduce_scatter | solution.py:183
  115.3 151.9 %all-gather.6.cloned.1.call-start = ((), (), s32[]{:S(2)}) async-start(), calls=%async_computation.7 | async-start | bytes 4718592 | tf_op jit(solution)/shard_map/all_gather | solution.py:146
  182.0 12.0 %collective-permute-start = (bf16[128,2048]{1,0:T(8,128)(2,1)}, bf16[128,2048]{1,0:T(8,128)(2,1)S(1)}, u32[]{:S(2)}, u32[]{:S(2)}) collective-permute-start(bf16[128,2048]{1,0:T(8,128)(2,1)} %add_convert_fusion.5), channel_id=1, source_target_pairs={{0,1},{2,3},{4,5},{6,7},{8,9},{10,11},{12,13},{14,15},{16,17},{18,... | collective-permute-start | bytes 1572872 | tf_op jit(solution)/shard_map/ppermute | solution.py:14
  199.7 4.5 %copy-start.18 = (pred[128,896]{1,0:T(8,128)(4,1)S(1)}, pred[128,896]{1,0:T(8,128)(4,1)}, u32[]{:S(2)}) copy-start(pred[128,896]{1,0:T(8,128)(4,1)} %get-tuple-element.19) | copy-start | bytes 344068
  204.2 6.8 %copy-start.9 = (bf16[768,512]{1,0:T(8,128)(2,1)S(1)}, bf16[768,512]{1,0:T(8,128)(2,1)}, u32[]{:S(2)}) copy-start(bf16[768,512]{1,0:T(8,128)(2,1)} %get-tuple-element.9) | copy-start | bytes 2359300
  204.2 6.8 %copy-start.28 = (bf16[1,8,512,128]{3,2,1,0:T(8,128)(2,1)S(1)}, bf16[1,8,512,128]{3,2,1,0:T(8,128)(2,1)}, u32[]{:S(2)}) copy-start(bf16[1,8,512,128]{3,2,1,0:T(8,128)(2,1)} %param.26) | copy-start | bytes 3145732
  214.7 4.3 %copy-start.22 = (f32[8,1,64]{2,0,1:T(8,128)S(1)}, f32[8,1,64]{2,0,1:T(8,128)}, u32[]{:S(2)}) copy-start(f32[8,1,64]{2,0,1:T(8,128)} %get-tuple-element.15) | copy-start | bytes 6148
  214.7 4.4 %copy-start.21 = (f32[8,1,64]{2,0,1:T(8,128)S(1)}, f32[8,1,64]{2,0,1:T(8,128)}, u32[]{:S(2)}) copy-start(f32[8,1,64]{2,0,1:T(8,128)} %get-tuple-element.16) | copy-start | bytes 6148
  218.7 102.1 %reduce-scatter.9.cloned.1.call-start = ((), (), s32[]{:S(2)}) async-start(), calls=%async_computation.8 | async-start | bytes 2359296 | tf_op jit(solution)/shard_map/reduce_scatter | solution.py:183
  267.2 7.8 %slice-start.6 = ((s8[5767168]{0:T(1024)(128)(4,1)}), s8[4194304]{0:T(1024)(128)(4,1)S(1)}, s32[]{:S(2)}) async-start(s8[5767168]{0:T(1024)(128)(4,1)} %bitcast.322), calls=%async_computation.16 | async-start | bytes 8388608
  270.7 4.4 %slice-start.7 = ((s8[5767168]{0:T(1024)(128)(4,1)}), s8[1572864]{0:T(1024)(128)(4,1)S(1)}, s32[]{:S(2)}) async-start(s8[5767168]{0:T(1024)(128)(4,1)} %bitcast.322), calls=%async_computation.17 | async-start | bytes 3145728
  271.4 6.6 %slice-start.2 = ((s8[5767168]{0:T(1024)(128)(4,1)}), s8[4194304]{0:T(1024)(128)(4,1)S(1)}, s32[]{:S(2)}) async-start(s8[5767168]{0:T(1024)(128)(4,1)} %bitcast.318), calls=%async_computation.12 | async-start | bytes 8388608
  285.8 71.9 %reduce-scatter.11.cloned.1.call-start = ((), (), s32[]{:S(2)}) async-start(), calls=%async_computation.9 | async-start | bytes 2359296 | tf_op jit(solution)/shard_map/reduce_scatter | solution.py:183
  292.5 68.4 %copy-start.1 = (bf16[1,2048,512]{2,1,0:T(8,128)(2,1)S(1)}, bf16[1,2048,512]{2,1,0:T(8,128)(2,1)}, u32[]{:S(2)}) copy-start(bf16[1,2048,512]{2,1,0:T(8,128)(2,1)} %param.28) | copy-start | bytes 6291460
  (27 other events, 70.2 us)
Sparse Core Ops, SparseCore 0:
  39.6 50.1 all-gather.3
  108.7 34.5 reduce-scatter.4
  145.6 34.3 reduce-scatter.6
  218.8 48.3 all-gather.5
  285.9 34.8 reduce-scatter.8
  323.0 34.6 reduce-scatter.10
where the time goes:
time: 374 us; the launch traced here: 368 us
  waiting for transfers between devices  212 us (57%)
  matrix products  81 us (22%)
  other arithmetic  29.1 us (8%)
  blocking collectives  16.3 us (4%)
  between operations  14.6 us (4%)
  local copies, waits for them, and re-layouts  10.7 us (3%)
  starting transfers between devices  4.1 us (1%)
    reduce_scatter x4, waiting for transfers between devices, shards(): lax.psum_scatter(total, 'expert', scatter_dimension=0, tiled=True)  130 us
    all_gather x2, waiting for transfers between devices, shards(): all_rows = lax.all_gather(whole_rows, 'expert', axis=0, tiled=True)  73.9 us
    all_gather x1, blocking collectives, shards(): lax.all_gather(jnp.swapaxes(shares_dense, 1, 2), 'expert', axis=1, tiled=...  16.3 us
    sub x2, other arithmetic, attend(): expd = jnp.where(visible[:, None, :], jnp.exp(scores - row_max), 0.0)  13.5 us
    dot_general x8, matrix products, shards(): jnp.einsum('jsr,jsd->jrd', place[:, e], down.reshape(sources, CAP, chunk)...  11.8 us
    dot_general x8, matrix products, shards(): jnp.dot(hidden_list[e], specialist_contract_factor[0, e][:, c * chunk:(c...  11.2 us
    dot_general x4, matrix products, shards(): jnp.dot(rows_in, specialist_switch_factor[0, e], preferred_element_type=j...  10.9 us
    dot_general x2, matrix products, attend(): jnp.einsum('thl,kl->thk', q_lat, key_rows, preferred_element_type=jnp.flo...  9.03 us
  transfers between devices with their start and end apart: 7, of which 7 were waited for; matrix products, arithmetic and copies ran while one was open for 6% of the time, Pallas kernels for 0%

commit v1 on v0

--- a/solution.py
+++ b/solution.py
@@ -6,6 +6,27 @@
 CAP = 64
 RETURN_CHUNKS = 2
 epsilon = 1e-06
+
+
+def gather_around(array, axis, dim):
+    peers, here, span = (lax.axis_size(axis), lax.axis_index(axis), array.shape[dim])
+    upward = [(i, (i + 1) % peers) for i in range(peers)]
+    downward = [(i, (i - 1) % peers) for i in range(peers)]
+    out = jnp.zeros((*array.shape[:dim], peers * span, *array.shape[dim + 1 :]), array.dtype)
+    out = lax.dynamic_update_slice_in_dim(out, array, here * span, axis=dim)
+    from_left = from_right = array
+    half = peers // 2
+    for turn in range(1, half + 1):
+        from_left = lax.ppermute(from_left, axis, upward)
+        out = lax.dynamic_update_slice_in_dim(
+            out, from_left, (here - turn) % peers * span, axis=dim
+        )
+        if turn < peers - half:
+            from_right = lax.ppermute(from_right, axis, downward)
+            out = lax.dynamic_update_slice_in_dim(
+                out, from_right, (here + turn) % peers * span, axis=dim
+            )
+    return out
 
 
 def shifted(value, axis, steps):
@@ -143,7 +164,7 @@
         whole_rows = lax.all_gather(moe_input, "tensor", axis=1, tiled=True)
         place = placed[step_index]
         share = slot_share[step_index]
-        all_rows = lax.all_gather(whole_rows, "expert", axis=0, tiled=True)
+        all_rows = gather_around(whole_rows, "expert", 0)
         all_rows = all_rows.reshape(sources, piece_list, full_width)
         hidden_list = []
         for e in range(expert_local):

time: 374 us -> 417 us (1.11)
  starting transfers between devices: 4.1 us -> 26.9 us
  local copies, waits for them, and re-layouts: 10.7 us -> 30.9 us
  waiting for transfers between devices: 212 us -> 205 us
  blocking collectives: 16.3 us -> 20.9 us
    all_gather x2 -> x0, waiting for transfers between devices: 73.9 us -> none  [shards(): all_rows = lax.all_gather(whole_rows, 'expert', axis=0, tiled=True)]
    ppermute x0 -> x14, waiting for transfers between devices: none -> 65 us  [the longest x8 64.9 us: gather_around(): from_left = lax.ppermute(from_left, axis, upward)]
    ppermute x0 -> x14, starting transfers between devices: none -> 22.9 us  [the longest x6 21.3 us: gather_around(): from_right = lax.ppermute(from_right, axis, downward)]
    dynamic_update_slice x0 -> x14, local copies, waits for them, and re-layouts: none -> 17.1 us  [the longest x8 8.83 us: gather_around(): lax.dynamic_update_slice_in_dim(out, from_left, (here - turn) % peers * s...]
    another operation x0 -> x2, local copies, waits for them, and re-layouts: none -> 5.04 us
    dot_general x4, matrix products: 7.47 us -> 12.4 us  [shards(): jnp.einsum('jsr,jrd->jsd', place[:, e], all_rows, preferred_element_type=...]
    all_gather x1, blocking collectives: 16.3 us -> 20.9 us  [shards(): lax.all_gather(jnp.swapaxes(shares_dense, 1, 2), 'expert', axis=1, tiled=...]
  transfers between devices with their start and end apart: 7 -> 19, of which waited for: 7 -> 12; matrix products, arithmetic and copies ran while one was open for 6% -> 9% of each run, Pallas kernels for 0% -> 0%
where the time goes in v1:
time: 417 us; the launch traced here: 409 us
  waiting for transfers between devices  205 us (49%)
  matrix products  81.9 us (20%)
  local copies, waits for them, and re-layouts  30.9 us (7%)
  other arithmetic  29.3 us (7%)
  starting transfers between devices  26.9 us (6%)
  blocking collectives  20.9 us (5%)
  between operations  14.2 us (3%)
    reduce_scatter x4, waiting for transfers between devices, shards(): lax.psum_scatter(total, 'expert', scatter_dimension=0, tiled=True)  131 us
    ppermute x8, waiting for transfers between devices, gather_around(): from_left = lax.ppermute(from_left, axis, upward)  64.9 us
    ppermute x6, starting transfers between devices, gather_around(): from_right = lax.ppermute(from_right, axis, downward)  21.3 us
    all_gather x1, blocking collectives, shards(): lax.all_gather(jnp.swapaxes(shares_dense, 1, 2), 'expert', axis=1, tiled=...  20.9 us
    sub x2, other arithmetic, attend(): expd = jnp.where(visible[:, None, :], jnp.exp(scores - row_max), 0.0)  13.5 us
    dot_general x4, matrix products, shards(): jnp.einsum('jsr,jrd->jsd', place[:, e], all_rows, preferred_element_type=...  12.4 us
    dot_general x8, matrix products, shards(): jnp.einsum('jsr,jsd->jrd', place[:, e], down.reshape(sources, CAP, chunk)...  11.6 us
    dot_general x8, matrix products, shards(): jnp.dot(hidden_list[e], specialist_contract_factor[0, e][:, c * chunk:(c...  11.2 us
  transfers between devices with their start and end apart: 19, of which 12 were waited for; matrix products, arithmetic and copies ran while one was open for 9% of the time, Pallas kernels for 0%

profile of v1, /device:TPU:0, one launch (start us, length us, event | category | flops | bytes accessed | tf_op | source)
XLA Modules:
  0.0 408.9 jit_solution(3589690113084134344)
XLA Ops:
  20.2 4.5 %fusion.105 = f32[128,8,896]{2,0,1:T(8,128)} fusion(bf16[1,8,128,512]{3,2,1,0:T(8,128)(2,1)S(1)} %copy-done.5, bf16[128,512]{1,0:T(8,128)(2,1)S(1)} %multiply_convert_fusion.3, bf16[768,512]{1,0:T(8,128)(2,1)} %get-tuple-element.14, bf16[16,8,8,128]{3,2,1,0:T(8,128)(2,1)S(1)} %fusion.130), kind=kOutput, calls=%fused_computation.97 | convolution fusion | flops 1076101120 | bytes 5898240 | tf_op jit(solution)/shard_map/thl,kl->thk/dot_general | solution.py:49
  24.8 6.7 %fusion.191 = (f32[128,8]{0,1:T(8,128)S(1)}, f32[128,8,896]{2,0,1:T(8,128)}) fusion(f32[128,8,896]{2,0,1:T(8,128)} %fusion.105, pred[128,896]{1,0:T(8,128)(4,1)} %get-tuple-element.24), kind=kOutput, calls=%fused_computation.220 | output fusion | flops 6423423 | bytes 7458816 | tf_op jit(solution)/shard_map/sub | solution.py:56
  31.5 3.9 fusion.126
  42.8 4.0 collective-permute-start.1
  46.9 20.9 %all-gather = f32[2,128,128]{2,1,0:T(8,128)S(1)} all-gather(f32[2,16,128]{2,1,0:T(8,128)S(1)} %bitcast.301), channel_id=2, replica_groups=mesh['groups'=2,'expert'=8,'section'=2,'tensor'=1] {'expert'}, dimensions={1}, use_global_device_ids=true | all-gather | bytes 147456 | tf_op jit(solution)/shard_map/all_gather | solution.py:103
  67.8 6.2 %slice_bitcast_fusion = (bf16[704,2048]{1,0:T(8,128)(2,1)}, bf16[704,2048]{1,0:T(8,128)(2,1)}) fusion(bf16[1,2,704,2048]{3,2,1,0:T(8,128)(2,1)} %param.33), kind=kLoop, calls=%fused_computation.40 | loop fusion | bytes 11534336 | tf_op jit(solution)/shard_map/squeeze | solution.py:193
  78.8 11.8 %collective-permute-done.2 = bf16[128,2048]{1,0:T(8,128)(2,1)} collective-permute-done((bf16[128,2048]{1,0:T(8,128)(2,1)}, bf16[128,2048]{1,0:T(8,128)(2,1)}, u32[]{:S(2)}, u32[]{:S(2)}) %collective-permute-start.2) | collective-permute-done | bytes 524320 | tf_op jit(solution)/shard_map/ppermute | solution.py:20
  99.8 6.9 %collective-permute-done.4 = bf16[128,2048]{1,0:T(8,128)(2,1)S(1)} collective-permute-done((bf16[128,2048]{1,0:T(8,128)(2,1)}, bf16[128,2048]{1,0:T(8,128)(2,1)S(1)}, u32[]{:S(2)}, u32[]{:S(2)}) %collective-permute-start.4) | collective-permute-done | bytes 524320 | tf_op jit(solution)/shard_map/ppermute | solution.py:20
  110.8 6.8 %collective-permute-done.6 = bf16[128,2048]{1,0:T(8,128)(2,1)S(1)} collective-permute-done((bf16[128,2048]{1,0:T(8,128)(2,1)S(1)}, bf16[128,2048]{1,0:T(8,128)(2,1)S(1)}, u32[]{:S(2)}, u32[]{:S(2)}) %collective-permute-start.6) | collective-permute-done | bytes 524320 | tf_op jit(solution)/shard_map/ppermute | solution.py:20
  118.4 3.5 convolution_convert_fusion.2
  144.0 28.6 %reduce-scatter.5.cloned.1.call-done = bf16[128,1024]{1,0:T(8,128)(2,1)} async-done(((bf16[1024,1024]{1,0:T(8,128)(2,1)}), bf16[128,1024]{1,0:T(8,128)(2,1)}) %reduce-scatter.5.cloned.1.call-update) | async-done | bytes 262160 | tf_op jit(solution)/shard_map/reduce_scatter | solution.py:204
  172.7 36.8 %reduce-scatter.7.cloned.1.call-done = bf16[128,1024]{1,0:T(8,128)(2,1)} async-done(((bf16[1024,1024]{1,0:T(8,128)(2,1)}), bf16[128,1024]{1,0:T(8,128)(2,1)}) %reduce-scatter.7.cloned.1.call-update) | async-done | bytes 262160 | tf_op jit(solution)/shard_map/reduce_scatter | solution.py:204
  214.9 8.7 %collective-permute-done.7 = bf16[128,2048]{1,0:T(8,128)(2,1)S(1)} collective-permute-done((bf16[128,2048]{1,0:T(8,128)(2,1)}, bf16[128,2048]{1,0:T(8,128)(2,1)S(1)}, u32[]{:S(2)}, u32[]{:S(2)}) %collective-permute-start.7) | collective-permute-done | bytes 524320 | tf_op jit(solution)/shard_map/ppermute | solution.py:35
  228.8 4.8 %fusion.107 = f32[128,8,896]{2,0,1:T(8,128)} fusion(bf16[1,8,128,512]{3,2,1,0:T(8,128)(2,1)} %param.25, bf16[128,512]{1,0:T(8,128)(2,1)S(1)} %multiply_convert_fusion.2, bf16[768,512]{1,0:T(8,128)(2,1)} %get-tuple-element.13, bf16[16,8,8,128]{3,2,1,0:T(8,128)(2,1)S(1)} %fusion.127), kind=kOutput, calls=%fused_computation.99 | convolution fusion | flops 1076101120 | bytes 5898240 | tf_op jit(solution)/shard_map/thl,kl->thk/dot_general | solution.py:49
  233.6 6.8 %fusion.192 = (f32[128,8]{0,1:T(8,128)S(1)}, f32[128,8,896]{2,0,1:T(8,128)}) fusion(f32[128,8,896]{2,0,1:T(8,128)} %fusion.107, pred[128,896]{1,0:T(8,128)(4,1)S(1)} %copy-done.15), kind=kOutput, calls=%fused_computation.221 | output fusion | flops 6423423 | bytes 7458816 | tf_op jit(solution)/shard_map/sub | solution.py:56
  240.4 3.7 fusion.125
  250.6 3.5 collective-permute-start.9
  254.1 11.6 %collective-permute-done.8 = bf16[128,2048]{1,0:T(8,128)(2,1)S(1)} collective-permute-done((bf16[128,2048]{1,0:T(8,128)(2,1)S(1)}, bf16[128,2048]{1,0:T(8,128)(2,1)S(1)}, u32[]{:S(2)}, u32[]{:S(2)}) %collective-permute-start.8) | collective-permute-done | bytes 524320 | tf_op jit(solution)/shard_map/ppermute | solution.py:20
  265.7 3.5 collective-permute-start.11
  269.4 12.1 %collective-permute-done.10 = bf16[128,2048]{1,0:T(8,128)(2,1)S(1)} collective-permute-done((bf16[128,2048]{1,0:T(8,128)(2,1)S(1)}, bf16[128,2048]{1,0:T(8,128)(2,1)S(1)}, u32[]{:S(2)}, u32[]{:S(2)}) %collective-permute-start.10) | collective-permute-done | bytes 524320 | tf_op jit(solution)/shard_map/ppermute | solution.py:20
  288.5 8.0 %collective-permute-done.12 = bf16[128,2048]{1,0:T(8,128)(2,1)S(1)} collective-permute-done((bf16[128,2048]{1,0:T(8,128)(2,1)S(1)}, bf16[128,2048]{1,0:T(8,128)(2,1)S(1)}, u32[]{:S(2)}, u32[]{:S(2)}) %collective-permute-start.12) | collective-permute-done | bytes 524320 | tf_op jit(solution)/shard_map/ppermute | solution.py:20
  299.3 7.8 %collective-permute-done.14 = bf16[128,2048]{1,0:T(8,128)(2,1)S(1)} collective-permute-done((bf16[128,2048]{1,0:T(8,128)(2,1)S(1)}, bf16[128,2048]{1,0:T(8,128)(2,1)S(1)}, u32[]{:S(2)}, u32[]{:S(2)}) %collective-permute-start.14) | collective-permute-done | bytes 524320 | tf_op jit(solution)/shard_map/ppermute | solution.py:20
  333.3 28.6 %reduce-scatter.9.cloned.1.call-done = bf16[128,1024]{1,0:T(8,128)(2,1)} async-done(((bf16[1024,1024]{1,0:T(8,128)(2,1)}), bf16[128,1024]{1,0:T(8,128)(2,1)}) %reduce-scatter.9.cloned.1.call-update) | async-done | bytes 262160 | tf_op jit(solution)/shard_map/reduce_scatter | solution.py:204
  361.9 36.9 %reduce-scatter.11.cloned.1.call-done = bf16[128,1024]{1,0:T(8,128)(2,1)} async-done(((bf16[1024,1024]{1,0:T(8,128)(2,1)}), bf16[128,1024]{1,0:T(8,128)(2,1)}) %reduce-scatter.11.cloned.1.call-update) | async-done | bytes 262160 | tf_op jit(solution)/shard_map/reduce_scatter | solution.py:204
  (196 shorter events, 117.9 us)
Async XLA Ops:
  6.5 166.1 %reduce-scatter.5.cloned.1.call-start = ((), (), s32[]{:S(2)}) async-start(), calls=%async_computation.4 | async-start | bytes 2359296 | tf_op jit(solution)/shard_map/reduce_scatter | solution.py:204
  38.6 8.2 %copy-start.19 = (s32[2,1,128,6]{2,1,3,0:T(1,128)S(1)}, s32[2,1,128,6]{2,1,3,0:T(1,128)}, u32[]{:S(2)}) copy-start(s32[2,1,128,6]{2,1,3,0:T(1,128)} %param.21) | copy-start | bytes 18436
  38.6 8.2 %copy-start.20 = (f32[2,1,128,6]{2,1,3,0:T(1,128)S(1)}, f32[2,1,128,6]{2,1,3,0:T(1,128)}, u32[]{:S(2)}) copy-start(f32[2,1,128,6]{2,1,3,0:T(1,128)} %param.22) | copy-start | bytes 18436
  42.3 32.7 %collective-permute-start = (bf16[128,2048]{1,0:T(8,128)(2,1)}, bf16[128,2048]{1,0:T(8,128)(2,1)}, u32[]{:S(2)}, u32[]{:S(2)}) collective-permute-start(bf16[128,2048]{1,0:T(8,128)(2,1)} %get-tuple-element.10), channel_id=1, source_target_pairs={{0,2},{2,4},{4,6},{6,8},{8,10},{10,12},{12,14},{14,0},{1,3},{3,5},... | collective-permute-start | bytes 1572872 | tf_op jit(solution)/shard_map/ppermute | solution.py:20
  42.8 32.6 %collective-permute-start.1 = (bf16[128,2048]{1,0:T(8,128)(2,1)}, bf16[128,2048]{1,0:T(8,128)(2,1)}, u32[]{:S(2)}, u32[]{:S(2)}) collective-permute-start(bf16[128,2048]{1,0:T(8,128)(2,1)} %get-tuple-element.10), channel_id=1, source_target_pairs={{0,14},{2,0},{4,2},{6,4},{8,6},{10,8},{12,10},{14,12},{1,15},{3,1}... | collective-permute-start | bytes 1572872 | tf_op jit(solution)/shard_map/ppermute | solution.py:25
  75.0 15.7 %collective-permute-start.2 = (bf16[128,2048]{1,0:T(8,128)(2,1)}, bf16[128,2048]{1,0:T(8,128)(2,1)}, u32[]{:S(2)}, u32[]{:S(2)}) collective-permute-start(bf16[128,2048]{1,0:T(8,128)(2,1)} %collective-permute-done), channel_id=1, source_target_pairs={{0,2},{2,4},{4,6},{6,8},{8,10},{10,12},{12,14},{14,0},{1,3},{3,5},... | collective-permute-start | bytes 1572872 | tf_op jit(solution)/shard_map/ppermute | solution.py:20
  75.4 19.1 %collective-permute-start.3 = (bf16[128,2048]{1,0:T(8,128)(2,1)}, bf16[128,2048]{1,0:T(8,128)(2,1)}, u32[]{:S(2)}, u32[]{:S(2)}) collective-permute-start(bf16[128,2048]{1,0:T(8,128)(2,1)} %collective-permute-done.1), channel_id=1, source_target_pairs={{0,14},{2,0},{4,2},{6,4},{8,6},{10,8},{12,10},{14,12},{1,15},{3,1}... | collective-permute-start | bytes 1572872 | tf_op jit(solution)/shard_map/ppermute | solution.py:25
  90.6 16.0 %collective-permute-start.4 = (bf16[128,2048]{1,0:T(8,128)(2,1)}, bf16[128,2048]{1,0:T(8,128)(2,1)S(1)}, u32[]{:S(2)}, u32[]{:S(2)}) collective-permute-start(bf16[128,2048]{1,0:T(8,128)(2,1)} %collective-permute-done.2), channel_id=1, source_target_pairs={{0,2},{2,4},{4,6},{6,8},{8,10},{10,12},{12,14},{14,0},{1,3},{3,5},... | collective-permute-start | bytes 1572872 | tf_op jit(solution)/shard_map/ppermute | solution.py:20
  94.5 15.5 %collective-permute-start.5 = (bf16[128,2048]{1,0:T(8,128)(2,1)}, bf16[128,2048]{1,0:T(8,128)(2,1)S(1)}, u32[]{:S(2)}, u32[]{:S(2)}) collective-permute-start(bf16[128,2048]{1,0:T(8,128)(2,1)} %collective-permute-done.3), channel_id=1, source_target_pairs={{0,14},{2,0},{4,2},{6,4},{8,6},{10,8},{12,10},{14,12},{1,15},{3,1}... | collective-permute-start | bytes 1572872 | tf_op jit(solution)/shard_map/ppermute | solution.py:25
  106.7 10.9 %collective-permute-start.6 = (bf16[128,2048]{1,0:T(8,128)(2,1)S(1)}, bf16[128,2048]{1,0:T(8,128)(2,1)S(1)}, u32[]{:S(2)}, u32[]{:S(2)}) collective-permute-start(bf16[128,2048]{1,0:T(8,128)(2,1)S(1)} %collective-permute-done.4), channel_id=1, source_target_pairs={{0,2},{2,4},{4,6},{6,8},{8,10},{10,12},{12,14},{14,0},{1,3},{3,5},... | collective-permute-start | bytes 1572872 | tf_op jit(solution)/shard_map/ppermute | solution.py:20
  117.6 7.2 %slice-start = ((s8[5767168]{0:T(1024)(128)(4,1)}), s8[4194304]{0:T(1024)(128)(4,1)S(1)}, s32[]{:S(2)}) async-start(s8[5767168]{0:T(1024)(128)(4,1)} %bitcast.312), calls=%async_computation.8 | async-start | bytes 8388608
  137.1 72.4 %reduce-scatter.7.cloned.1.call-start = ((), (), s32[]{:S(2)}) async-start(), calls=%async_computation.5 | async-start | bytes 2359296 | tf_op jit(solution)/shard_map/reduce_scatter | solution.py:204
  144.0 217.9 %reduce-scatter.9.cloned.1.call-start = ((), (), s32[]{:S(2)}) async-start(), calls=%async_computation.6 | async-start | bytes 2359296 | tf_op jit(solution)/shard_map/reduce_scatter | solution.py:204
  211.4 12.1 %collective-permute-start.7 = (bf16[128,2048]{1,0:T(8,128)(2,1)}, bf16[128,2048]{1,0:T(8,128)(2,1)S(1)}, u32[]{:S(2)}, u32[]{:S(2)}) collective-permute-start(bf16[128,2048]{1,0:T(8,128)(2,1)} %add_convert_fusion.5), channel_id=1, source_target_pairs={{0,1},{2,3},{4,5},{6,7},{8,9},{10,11},{12,13},{14,15},{16,17},{18,... | collective-permute-start | bytes 1572872 | tf_op jit(solution)/shard_map/ppermute | solution.py:35
  250.6 15.1 %collective-permute-start.8 = (bf16[128,2048]{1,0:T(8,128)(2,1)S(1)}, bf16[128,2048]{1,0:T(8,128)(2,1)S(1)}, u32[]{:S(2)}, u32[]{:S(2)}) collective-permute-start(bf16[128,2048]{1,0:T(8,128)(2,1)S(1)} %get-tuple-element.6), channel_id=1, source_target_pairs={{0,2},{2,4},{4,6},{6,8},{8,10},{10,12},{12,14},{14,0},{1,3},{3,5},... | collective-permute-start | bytes 1572872 | tf_op jit(solution)/shard_map/ppermute | solution.py:20
  250.6 15.1 %collective-permute-start.9 = (bf16[128,2048]{1,0:T(8,128)(2,1)S(1)}, bf16[128,2048]{1,0:T(8,128)(2,1)}, u32[]{:S(2)}, u32[]{:S(2)}) collective-permute-start(bf16[128,2048]{1,0:T(8,128)(2,1)S(1)} %get-tuple-element.6), channel_id=1, source_target_pairs={{0,14},{2,0},{4,2},{6,4},{8,6},{10,8},{12,10},{14,12},{1,15},{3,1}... | collective-permute-start | bytes 1572872 | tf_op jit(solution)/shard_map/ppermute | solution.py:25
  265.7 15.8 %collective-permute-start.10 = (bf16[128,2048]{1,0:T(8,128)(2,1)S(1)}, bf16[128,2048]{1,0:T(8,128)(2,1)S(1)}, u32[]{:S(2)}, u32[]{:S(2)}) collective-permute-start(bf16[128,2048]{1,0:T(8,128)(2,1)S(1)} %collective-permute-done.8), channel_id=1, source_target_pairs={{0,2},{2,4},{4,6},{6,8},{8,10},{10,12},{12,14},{14,0},{1,3},{3,5},... | collective-permute-start | bytes 1572872 | tf_op jit(solution)/shard_map/ppermute | solution.py:20
  265.7 18.5 %collective-permute-start.11 = (bf16[128,2048]{1,0:T(8,128)(2,1)}, bf16[128,2048]{1,0:T(8,128)(2,1)S(1)}, u32[]{:S(2)}, u32[]{:S(2)}) collective-permute-start(bf16[128,2048]{1,0:T(8,128)(2,1)} %collective-permute-done.9), channel_id=1, source_target_pairs={{0,14},{2,0},{4,2},{6,4},{8,6},{10,8},{12,10},{14,12},{1,15},{3,1}... | collective-permute-start | bytes 1572872 | tf_op jit(solution)/shard_map/ppermute | solution.py:25
  281.5 15.1 %collective-permute-start.12 = (bf16[128,2048]{1,0:T(8,128)(2,1)S(1)}, bf16[128,2048]{1,0:T(8,128)(2,1)S(1)}, u32[]{:S(2)}, u32[]{:S(2)}) collective-permute-start(bf16[128,2048]{1,0:T(8,128)(2,1)S(1)} %collective-permute-done.10), channel_id=1, source_target_pairs={{0,2},{2,4},{4,6},{6,8},{8,10},{10,12},{12,14},{14,0},{1,3},{3,5},... | collective-permute-start | bytes 1572872 | tf_op jit(solution)/shard_map/ppermute | solution.py:20
  284.2 14.2 %collective-permute-start.13 = (bf16[128,2048]{1,0:T(8,128)(2,1)S(1)}, bf16[128,2048]{1,0:T(8,128)(2,1)S(1)}, u32[]{:S(2)}, u32[]{:S(2)}) collective-permute-start(bf16[128,2048]{1,0:T(8,128)(2,1)S(1)} %collective-permute-done.11), channel_id=1, source_target_pairs={{0,14},{2,0},{4,2},{6,4},{8,6},{10,8},{12,10},{14,12},{1,15},{3,1}... | collective-permute-start | bytes 1572872 | tf_op jit(solution)/shard_map/ppermute | solution.py:25
  296.5 10.6 %collective-permute-start.14 = (bf16[128,2048]{1,0:T(8,128)(2,1)S(1)}, bf16[128,2048]{1,0:T(8,128)(2,1)S(1)}, u32[]{:S(2)}, u32[]{:S(2)}) collective-permute-start(bf16[128,2048]{1,0:T(8,128)(2,1)S(1)} %collective-permute-done.12), channel_id=1, source_target_pairs={{0,2},{2,4},{4,6},{6,8},{8,10},{10,12},{12,14},{14,0},{1,3},{3,5},... | collective-permute-start | bytes 1572872 | tf_op jit(solution)/shard_map/ppermute | solution.py:20
  297.6 16.5 %slice-start.2 = ((s8[5767168]{0:T(1024)(128)(4,1)}), s8[4194304]{0:T(1024)(128)(4,1)S(1)}, s32[]{:S(2)}) async-start(s8[5767168]{0:T(1024)(128)(4,1)} %bitcast.314), calls=%async_computation.10 | async-start | bytes 8388608
  326.5 72.3 %reduce-scatter.11.cloned.1.call-start = ((), (), s32[]{:S(2)}) async-start(), calls=%async_computation.7 | async-start | bytes 2359296 | tf_op jit(solution)/shard_map/reduce_scatter | solution.py:204
  333.3 68.8 %copy-start.1 = (bf16[1,2048,512]{2,1,0:T(8,128)(2,1)S(1)}, bf16[1,2048,512]{2,1,0:T(8,128)(2,1)}, u32[]{:S(2)}) copy-start(bf16[1,2048,512]{2,1,0:T(8,128)(2,1)} %param.28) | copy-start | bytes 6291460
  (33 other events, 116.1 us)
Sparse Core Ops, SparseCore 0:
  137.2 35.4 reduce-scatter.4
  175.0 34.4 reduce-scatter.6
  326.6 35.2 reduce-scatter.8
  364.1 34.6 reduce-scatter.10
